TPU v7x, 256 devices: a whole 4x4x8 slice. The times are simulated.
256 devices in a mesh: section: 16 (over y_hi, x, core), ray: 8 (over z), dp: 2 (over y_lo).
Axes of the slice: x: 4, y: 4 (y_hi: 2, y_lo: 2; y = y_hi * 2 + y_lo), z: 8, core: 2. Of those that a mesh axis runs over, the one named last changes fastest.
Arguments:
- section_tokens: bfloat16 [16, 2, 1024, 1024], P('section', 'dp', 'ray'), may hold values from -6 to 6
- enc_ln1: float32 [16, 1024], P('section'), may hold values from 0.5 to 1.5
- enc_qkv: bfloat16 [16, 1024, 3, 1024], P('section', None, None, 'ray'), may hold values from -40 to 40
- enc_out: bfloat16 [16, 1024, 1024], P('section', 'ray'), may hold values from -0.1875 to 0.1875
- enc_ln2: float32 [16, 1024], P('section'), may hold values from 0.5 to 1.5
- enc_up: bfloat16 [16, 1024, 4096], P('section', None, 'ray'), may hold values from -0.1875 to 0.1875
- enc_down: bfloat16 [16, 4096, 1024], P('section', 'ray'), may hold values from -0.09375 to 0.09375
- set_latent: bfloat16 [2, 1024, 1024], P('dp', 'ray'), may hold values from -6 to 6
- ray_queries: bfloat16 [2, 32768, 1024], P('dp', ('section', 'ray')), may hold values from -6 to 6
- dec_query: bfloat16 [1024, 1024], P('section'), may hold values from -40 to 40
- dec_kv: bfloat16 [1024, 2, 1024], P('section'), may hold values from -1 to 1
- dec_out: bfloat16 [1024, 1024], P('section'), may hold values from -0.1875 to 0.1875
- feature_grad: bfloat16 [2, 32768, 1024], P('dp', ('section', 'ray')), may hold values from -2 to 2
Outputs:
- handed: bfloat16 [16, 2, 1024, 1024], P('section', 'dp', 'ray')
- finished: bfloat16 [2, 1024, 1024], P('dp', 'ray', 'section')
- ray_features: bfloat16 [2, 32768, 1024], P('dp', ('section', 'ray'))
- latent_grad: bfloat16 [2, 1024, 1024], P('dp', 'ray')
- out_grad: float32 [1024, 1024], replicated
All inputs are finite; a program needn't handle non-finite values.
Results may differ from a plain program's by a relative error of at most 0.022.
The roundings to bfloat16 on the way count: a program that leaves them out, or rounds other values in their place, can miss the bound.
Values may be sent and summed in bfloat16 or wider, within the bound.
No kernel may reach another device: no remote copies, remote signals or barrier semaphores. Data moves between devices by JAX's collectives and lax.ppermute only.
A program may use at most 128 MiB of HBM per device.

v0:
```python
import math
import jax
import jax.numpy as jnp
from jax import lax
from jax.sharding import PartitionSpec as P

HEADS = 16


def shifted(value, axis, by):
    count = lax.axis_size(axis)
    pairs = [(i, i + by) for i in range(count) if 0 <= i + by < count]
    return lax.ppermute(value, axis, pairs)


def spread_2(value, axis, root):
    mine = lax.axis_index(axis) == root
    return lax.psum(jnp.where(mine, value, jnp.zeros_like(value)), axis)


def layer_norm(values, gain):
    values = values.astype(jnp.float32)
    center = values - jnp.mean(values, -1, keepdims=True)
    spread = jnp.mean(center * center, -1, keepdims=True)
    return center * lax.rsqrt(spread + 1e-05) * gain


def softmax_rows(scores):
    top = jnp.max(scores, -1, keepdims=True)
    expo = jnp.exp(scores - top)
    return expo / jnp.sum(expo, -1, keepdims=True)


def attend_heads(packed, head_dim):
    length = packed.shape[0]
    heads = packed.shape[1] // (3 * head_dim)
    split = packed.reshape(length, 3, heads, head_dim)
    scores = jnp.einsum(
        "qhd,khd->hqk", split[:, 0], split[:, 1], preferred_element_type=jnp.float32
    ) / math.sqrt(head_dim)
    probs = softmax_rows(scores).astype(jnp.bfloat16)
    mixed = jnp.einsum("hqk,khd->qhd", probs, split[:, 2], preferred_element_type=jnp.float32)
    return mixed.astype(jnp.bfloat16).reshape(length, heads * head_dim)


def latent_rows(pair_sum, w_pairs):
    result = lax.dot_general(
        pair_sum[:, 0],
        w_pairs[:, 0, :],
        (((1,), (1,)), ((), ())),
        preferred_element_type=jnp.float32,
    )
    result = result + lax.dot_general(
        pair_sum[:, 1],
        w_pairs[:, 1, :],
        (((1,), (1,)), ((), ())),
        preferred_element_type=jnp.float32,
    )
    return result.astype(jnp.bfloat16)


def local(
    section_tokens,
    enc_ln1,
    enc_qkv,
    enc_out,
    enc_ln2,
    enc_up,
    enc_down,
    set_latent,
    ray_queries,
    dec_query,
    dec_kv,
    dec_out,
    feature_grad,
):
    tokens = section_tokens[0, 0]
    width = tokens.shape[1]
    head_dim = width // HEADS
    local_width = enc_out.shape[1]
    w_qkv = enc_qkv[0].reshape(width, 3 * local_width)
    w_attn_out = enc_out[0]
    w_upper = enc_up[0]
    w_lower = enc_down[0]
    gain_one = enc_ln1[0]
    gain_two = enc_ln2[0]
    normed = layer_norm(tokens, gain_one).astype(jnp.bfloat16)
    packed = jnp.dot(
        lax.all_gather(normed, "ray", axis=0, tiled=True), w_qkv, preferred_element_type=jnp.float32
    ).astype(jnp.bfloat16)
    mixed = attend_heads(packed, head_dim)
    attn_rows = lax.psum_scatter(
        jnp.dot(mixed, w_attn_out, preferred_element_type=jnp.float32).astype(jnp.bfloat16),
        "ray",
        scatter_dimension=0,
        tiled=True,
    ).astype(jnp.float32)
    hidden = (tokens.astype(jnp.float32) + attn_rows).astype(jnp.bfloat16)
    upper = jax.nn.gelu(
        jnp.dot(
            lax.all_gather(
                layer_norm(hidden, gain_two).astype(jnp.bfloat16), "ray", axis=0, tiled=True
            ),
            w_upper,
            preferred_element_type=jnp.float32,
        ),
        approximate=True,
    ).astype(jnp.bfloat16)
    lower_rows = lax.psum_scatter(
        jnp.dot(upper, w_lower, preferred_element_type=jnp.float32).astype(jnp.bfloat16),
        "ray",
        scatter_dimension=0,
        tiled=True,
    ).astype(jnp.float32)
    layer_out = (hidden.astype(jnp.float32) + lower_rows).astype(jnp.bfloat16)
    handed = shifted(layer_out, "section", 1)
    finished_all = spread_2(layer_out, "section", lax.axis_size("section") - 1)
    columns = width // lax.axis_size("section")
    finished = lax.dynamic_slice_in_dim(
        finished_all, lax.axis_index("section") * columns, columns, 1
    )
    w_query, w_pairs, w_mix = (
        lax.all_gather(dec_query, "section", axis=0, tiled=True),
        lax.all_gather(dec_kv, "section", axis=0, tiled=True),
        lax.all_gather(dec_out, "section", axis=0, tiled=True),
    )
    latent = set_latent[0]
    queries = ray_queries[0]
    cotangent = feature_grad[0]
    flat_pairs = w_pairs.reshape(width, 2 * width)
    key_values = lax.all_gather(
        jnp.dot(latent, flat_pairs, preferred_element_type=jnp.float32).astype(jnp.bfloat16),
        "ray",
        axis=0,
        tiled=True,
    )
    scene_len = key_values.shape[0]
    ray_rows = queries.shape[0]
    scale = 1.0 / math.sqrt(head_dim)
    keys = key_values[:, :width].reshape(scene_len, HEADS, head_dim)
    values = key_values[:, width:].reshape(scene_len, HEADS, head_dim)
    query = (
        jnp.dot(queries, w_query, preferred_element_type=jnp.float32)
        .astype(jnp.bfloat16)
        .reshape(ray_rows, HEADS, head_dim)
    )
    scores = jnp.einsum("rhd,lhd->hrl", query, keys, preferred_element_type=jnp.float32) * scale
    probs = softmax_rows(scores)
    probs_low = probs.astype(jnp.bfloat16)
    attended = (
        jnp.einsum("hrl,lhd->rhd", probs_low, values, preferred_element_type=jnp.float32)
        .astype(jnp.bfloat16)
        .reshape(ray_rows, width)
    )
    features = (
        queries.astype(jnp.float32) + jnp.dot(attended, w_mix, preferred_element_type=jnp.float32)
    ).astype(jnp.bfloat16)
    mix_term = lax.dot_general(
        attended, cotangent, (((0,), (0,)), ((), ())), preferred_element_type=jnp.float32
    )
    out_grad = lax.psum(mix_term, ("section", "ray", "dp"))
    attn_grad = lax.dot_general(
        cotangent, w_mix, (((1,), (1,)), ((), ())), preferred_element_type=jnp.float32
    )
    attn_grad = attn_grad.astype(jnp.bfloat16).reshape(ray_rows, HEADS, head_dim)
    prob_grad = jnp.einsum("rhd,lhd->hrl", attn_grad, values, preferred_element_type=jnp.float32)
    delta = jnp.sum(probs * prob_grad, -1, keepdims=True)
    score_grad = (probs * (prob_grad - delta) * scale).astype(jnp.bfloat16)
    count = latent.shape[0] * lax.axis_size("ray")
    key_grad = jnp.einsum(
        "hrl,rhd->lhd", score_grad, query, preferred_element_type=jnp.float32
    ).reshape(count, width)
    value_grad = jnp.einsum(
        "hrl,rhd->lhd", probs_low, attn_grad, preferred_element_type=jnp.float32
    ).reshape(count, width)
    stacked = jnp.stack([key_grad, value_grad], 1)
    pair_rows = lax.psum_scatter(
        stacked.astype(jnp.bfloat16), "ray", scatter_dimension=0, tiled=True
    )
    pair_sum = lax.psum(pair_rows, "section")
    latent_grad = latent_rows(pair_sum, w_pairs)
    return (handed[None, None], finished[None], features[None], latent_grad[None], out_grad)


def solution(mesh):
    return jax.shard_map(
        local,
        mesh=mesh,
        in_specs=(
            P("section", "dp", "ray", None),
            P("section", None),
            P("section", None, None, "ray"),
            P("section", "ray", None),
            P("section", None),
            P("section", None, "ray"),
            P("section", "ray", None),
            P("dp", "ray", None),
            P("dp", ("section", "ray"), None),
            P("section", None),
            P("section", None, None),
            P("section", None),
            P("dp", ("section", "ray"), None),
        ),
        out_specs=(
            P("section", "dp", "ray", None),
            P("dp", "ray", "section"),
            P("dp", ("section", "ray"), None),
            P("dp", "ray", None),
            P(),
        ),
        check_vma=False,
    )
```

profile of v0, /device:TPU:2, one launch (start us, length us, event | category | flops | bytes accessed | tf_op | source)
XLA Modules:
  0.0 928.3 jit_solution(4946242236666145838)
XLA Ops:
  8.1 1.1 convert_reduce_fusion.1
  9.2 1.2 fusion.73
  10.4 1.9 fusion.75
  12.3 0.0 reduce-scatter.6.cloned.1.call-start
  12.4 1.4 copy.44
  13.8 42.5 %all-gather.7.cloned.1.call-done = bf16[1024,1024]{1,0:T(8,128)(2,1)} async-done(((bf16[128,1024]{1,0:T(8,128)(2,1)}), bf16[1024,1024]{1,0:T(8,128)(2,1)}) %all-gather.7.cloned.1.call-update) | async-done | bytes 2097168 | tf_op jit(solution)/shard_map/all_gather | solution.py:89
  56.3 2.6 convolution_convert_fusion.3
  58.9 4.9 fusion.97
  63.7 4.3 fusion.48
  68.1 2.1 convolution_convert_fusion.2
  70.1 0.0 all-gather.11.cloned.1.call-start
  70.2 0.5 all-gather.11.cloned.1.call-update
  70.7 0.0 all-gather.15.cloned.1.call-start
  70.8 0.5 all-gather.15.cloned.1.call-update
  71.3 0.0 all-gather.17.cloned.1.call-start
  71.4 0.5 all-gather.17.cloned.1.call-update
  71.9 0.0 all-gather.9.cloned.1.call-start
  71.9 39.7 %reduce-scatter.6.cloned.1.call-done = bf16[128,1024]{1,0:T(8,128)(2,1)} async-done(((bf16[1024,1024]{1,0:T(8,128)(2,1)}), bf16[128,1024]{1,0:T(8,128)(2,1)}) %reduce-scatter.6.cloned.1.call-update) | async-done | bytes 262160 | tf_op jit(solution)/shard_map/reduce_scatter | solution.py:92
  111.7 1.1 convert_reduce_fusion
  112.8 0.2 fusion.70
  113.0 0.9 fusion.72
  114.0 0.0 all-gather.13.cloned.1.call-start
  114.0 18.6 %all-gather.11.cloned.1.call-done = bf16[1024,2,1024]{2,1,0:T(2,128)(2,1)} async-done(((bf16[64,2,1024]{2,1,0:T(2,128)(2,1)}), bf16[1024,2,1024]{2,1,0:T(2,128)(2,1)}) %all-gather.11.cloned.1.call-update) | async-done | bytes 4194320 | tf_op jit(solution)/shard_map/all_gather | solution.py:124
  132.7 11.1 %copy.47 = bf16[1024,2,1024]{0,2,1:T(8,128)(2,1)} copy(bf16[1024,2,1024]{2,1,0:T(2,128)(2,1)} %all-gather.11.cloned.1.call-done) | data formatting | bytes 8388608 | tf_op jit(solution)/shard_map/all_gather | solution.py:124
  143.8 4.6 convolution_convert_fusion
  148.5 0.0 reduce-scatter.8.cloned.1.call-start
  148.5 39.0 %all-gather.15.cloned.1.call-done = bf16[1024,1024]{1,0:T(8,128)(2,1)} async-done(((bf16[64,1024]{1,0:T(8,128)(2,1)}), bf16[1024,1024]{1,0:T(8,128)(2,1)}) %all-gather.15.cloned.1.call-update) | async-done | bytes 2097168 | tf_op jit(solution)/shard_map/all_gather | solution.py:123
  187.5 2.3 convolution_convert_fusion.5
  189.8 1.0 copy.49
  190.8 51.5 %all-gather.17.cloned.1.call-done = bf16[1024,1024]{1,0:T(8,128)(2,1)} async-done(((bf16[64,1024]{1,0:T(8,128)(2,1)}), bf16[1024,1024]{1,0:T(8,128)(2,1)}) %all-gather.17.cloned.1.call-update) | async-done | bytes 2097168 | tf_op jit(solution)/shard_map/all_gather | solution.py:125
  242.3 2.3 convolution_convert_fusion.4
  244.6 1.0 copy.51
  245.6 39.2 %all-gather.9.cloned.1.call-done = bf16[1024,1024]{1,0:T(8,128)(2,1)} async-done(((bf16[128,1024]{1,0:T(8,128)(2,1)}), bf16[1024,1024]{1,0:T(8,128)(2,1)}) %all-gather.9.cloned.1.call-update) | async-done | bytes 2097168 | tf_op jit(solution)/shard_map/all_gather | solution.py:101
  284.9 5.8 convolution_convert_fusion.1
  290.7 0.2 reduce-scatter.10.cloned.1.call-start
  290.9 66.2 %all-gather.13.cloned.1.call-done = bf16[1024,2048]{1,0:T(8,128)(2,1)} async-done(((bf16[128,2048]{1,0:T(8,128)(2,1)}), bf16[1024,2048]{1,0:T(8,128)(2,1)}) %all-gather.13.cloned.1.call-update) | async-done | bytes 4194320 | tf_op jit(solution)/shard_map/all_gather | solution.py:131
  357.2 4.0 fusion.96
  361.2 2.6 copy.50
  363.8 2.9 copy.48
  366.7 9.8 %fusion.98 = (f32[16,256]{1,0:T(8,128)S(1)}, f32[16,256,1024]{2,1,0:T(8,128)}) fusion(bf16[256,16,64]{0,2,1:T(8,128)(2,1)S(1)} %bitcast.149, bf16[1024,16,64]{0,2,1:T(8,128)(2,1)} %bitcast.144), kind=kOutput, calls=%fused_computation.110 | convolution fusion | flops 549454848 | bytes 19415040 | tf_op jit(solution)/shard_map/sub | solution.py:30
  376.5 8.1 fusion.99
  384.5 38.2 %fusion.38 = bf16[16,64,1024]{2,1,0:T(8,128)(2,1)} fusion(bf16[256,16,64]{0,2,1:T(8,128)(2,1)S(1)} %bitcast.150, f32[16,256,1024]{2,1,0:T(8,128)} %fusion.99, f32[16,256,1024]{2,1,0:T(8,128)} %get-tuple-element.18, f32[16,256]{1,0:T(8,128)S(1)} %get-tuple-element.17), kind=kOutput, calls=%fused_computation.40 | convolution fusion | flops 567284736 | bytes 36192256 | tf_op jit(solution)/shard_map/hrl,rhd->lhd/dot_general | solution.py:170
  422.8 7.1 fusion.35
  429.9 2.4 pad_maximum_fusion
  432.3 6.5 copy.57
  438.8 0.0 all-reduce.6.cloned.1.call-start
  438.9 1.9 broadcast_select_fusion
  440.8 52.2 %reduce-scatter.10.cloned.1.call-done = bf16[128,2048]{1,0:T(8,128)(2,1)} async-done(((bf16[1024,2048]{1,0:T(8,128)(2,1)}), bf16[128,2048]{1,0:T(8,128)(2,1)}) %reduce-scatter.10.cloned.1.call-update) | async-done | bytes 524304
  492.9 2.0 copy.58
  495.0 0.3 all-reduce.4.cloned.1.call-start
  495.3 8.5 fusion.42
  503.8 2.7 fusion.78
  506.5 10.0 %fusion.95 = (bf16[1024,1,1024]{2,1,0:T(2,128)(2,1)}, bf16[1024,1,1024]{2,1,0:T(2,128)(2,1)}) fusion(bf16[1024,2,1024]{2,1,0:T(2,128)(2,1)} %all-gather.11.cloned.1.call-done), kind=kLoop, calls=%fused_computation.107 | loop fusion | bytes 8388608 | tf_op jit(solution)/shard_map/slice | solution.py:49
  516.5 1.9 collective-permute-start
  518.5 1.5 fusion.45
  520.0 4.7 collective-permute-done
  524.7 109.9 %all-reduce.6.cloned.1.call-done = (bf16[128,1024]{1,0:T(8,128)(2,1)}, bf16[128,2,1024]{0,2,1:T(8,128)(2,1)}) async-done(((bf16[128,1024]{1,0:T(8,128)(2,1)}, bf16[128,2,1024]{0,2,1:T(8,128)(2,1)}), (bf16[128,1024]{1,0:T(8,128)(2,1)}, bf16[128,2,1024]{0,2,1:T(8,128)(2,1)})) %all-reduce.6.cloned.1.call-update) | async-done | bytes 786448 | tf_op jit(solution)/shard_map/psum | solution.py:18
  634.6 0.8 constant_dynamic-slice_fusion
  635.5 0.7 copy.46
  636.2 3.1 fusion.33
  639.3 3.9 fusion.49
  643.2 272.5 %all-reduce.4.cloned.1.call-done = f32[1024,1024]{1,0:T(8,128)} async-done(((f32[1024,1024]{1,0:T(8,128)}), f32[1024,1024]{1,0:T(8,128)}) %all-reduce.4.cloned.1.call-update) | async-done | bytes 4194320 | tf_op jit(solution)/shard_map/psum | solution.py:161
  915.7 0.7 copy.75
  916.4 4.8 copy.76
  (44 shorter events, 0.3 us)
Async XLA Ops:
  8.0 276.9 %copy-start = (bf16[1,512,1024]{2,1,0:T(8,128)(2,1)S(1)}, bf16[1,512,1024]{2,1,0:T(8,128)(2,1)}, u32[]{:S(2)}) copy-start(bf16[1,512,1024]{2,1,0:T(8,128)(2,1)} %param.19) | copy-start | bytes 3145732
  8.0 48.2 %all-gather.7.cloned.1.call-start = ((), (), s32[]{:S(2)}) async-start(), calls=%async_computation.3 | async-start | bytes 2359296 | tf_op jit(solution)/shard_map/all_gather | solution.py:89
  12.3 99.4 %reduce-scatter.6.cloned.1.call-start = ((), (), s32[]{:S(2)}) async-start(), calls=%async_computation.4 | async-start | bytes 2359296 | tf_op jit(solution)/shard_map/reduce_scatter | solution.py:92
  63.7 4.3 copy-start.11
  68.0 43.6 %copy-start.2 = (bf16[1,1,128,1024]{3,2,1,0:T(8,128)(2,1)S(1)}, bf16[1,1,128,1024]{3,2,1,0:T(8,128)(2,1)}, u32[]{:S(2)}) copy-start(bf16[1,1,128,1024]{3,2,1,0:T(8,128)(2,1)} %param.13) | copy-start | bytes 786436
  68.0 45.0 %copy-start.14 = (f32[1,1024]{1,0:T(1,128)S(1)}, f32[1,1024]{1,0:T(1,128)}, u32[]{:S(2)}) copy-start(f32[1,1024]{1,0:T(1,128)} %param.17) | copy-start | bytes 12292
  70.1 62.5 %all-gather.11.cloned.1.call-start = ((), (), s32[]{:S(2)}) async-start(), calls=%async_computation.7 | async-start | bytes 4456448 | tf_op jit(solution)/shard_map/all_gather | solution.py:124
  70.7 116.8 %all-gather.15.cloned.1.call-start = ((), (), s32[]{:S(2)}) async-start(), calls=%async_computation.9 | async-start | bytes 2228224 | tf_op jit(solution)/shard_map/all_gather | solution.py:123
  71.3 171.0 %all-gather.17.cloned.1.call-start = ((), (), s32[]{:S(2)}) async-start(), calls=%async_computation.10 | async-start | bytes 2228224 | tf_op jit(solution)/shard_map/all_gather | solution.py:125
  71.9 213.0 %all-gather.9.cloned.1.call-start = ((), (), s32[]{:S(2)}) async-start(), calls=%async_computation.5 | async-start | bytes 2359296 | tf_op jit(solution)/shard_map/all_gather | solution.py:101
  114.0 29.8 %copy-start.12 = (bf16[1,128,1024]{2,1,0:T(8,128)(2,1)S(1)}, bf16[1,128,1024]{2,1,0:T(8,128)(2,1)}, u32[]{:S(2)}) copy-start(bf16[1,128,1024]{2,1,0:T(8,128)(2,1)} %param.20) | copy-start | bytes 786436
  114.0 243.2 %all-gather.13.cloned.1.call-start = ((), (), s32[]{:S(2)}) async-start(), calls=%async_computation.8 | async-start | bytes 4718592 | tf_op jit(solution)/shard_map/all_gather | solution.py:131
  143.8 43.7 %copy-start.8 = (bf16[1,256,1024]{2,1,0:T(8,128)(2,1)S(1)}, bf16[1,256,1024]{2,1,0:T(8,128)(2,1)}, u32[]{:S(2)}) copy-start(bf16[1,256,1024]{2,1,0:T(8,128)(2,1)} %param.21) | copy-start | bytes 1572868
  143.8 98.5 %copy-start.6 = (bf16[1,256,1024]{2,1,0:T(8,128)(2,1)S(1)}, bf16[1,256,1024]{2,1,0:T(8,128)(2,1)}, u32[]{:S(2)}) copy-start(bf16[1,256,1024]{2,1,0:T(8,128)(2,1)} %param.25) | copy-start | bytes 1572868
  148.5 290.5 %reduce-scatter.8.cloned.1.call-start = ((), (), s32[]{:S(2)}) async-start(), calls=%async_computation.6 | async-start | bytes 2359296 | tf_op jit(solution)/shard_map/reduce_scatter | solution.py:109
  290.7 202.2 %reduce-scatter.10.cloned.1.call-start = ((), (), s32[]{:S(2)}) async-start(), calls=%async_computation.12 | async-start | bytes 4718592
  361.2 5.4 copy-start.10
  366.6 9.8 %copy-start.4 = (bf16[256,1024]{0,1:T(8,128)(2,1)S(1)}, bf16[256,1024]{0,1:T(8,128)(2,1)}, u32[]{:S(2)}) copy-start(bf16[256,1024]{0,1:T(8,128)(2,1)} %copy.51) | copy-start | bytes 1572868
  422.8 7.1 copy-start.5
  438.8 195.8 %all-reduce.6.cloned.1.call-start = ((), (), s32[]{:S(2)}) async-start(), calls=%async_computation.13 | async-start | bytes 1572864 | tf_op jit(solution)/shard_map/psum | solution.py:18
  495.0 8.8 copy-start.7
  495.0 420.7 %all-reduce.4.cloned.1.call-start = ((), (), s32[]{:S(2)}) async-start(), calls=%async_computation.11 | async-start | bytes 8388608 | tf_op jit(solution)/shard_map/psum | solution.py:161
  506.5 10.0 %copy-start.13 = (bf16[128,1024]{1,0:T(8,128)(2,1)S(1)}, bf16[128,1024]{1,0:T(8,128)(2,1)}, u32[]{:S(2)}) copy-start(bf16[128,1024]{1,0:T(8,128)(2,1)} %get-tuple-element.8) | copy-start | bytes 786436
  506.5 11.9 %copy-start.3 = (bf16[1024,1024]{1,0:T(8,128)(2,1)S(1)}, bf16[1024,1024]{1,0:T(8,128)(2,1)}, u32[]{:S(2)}) copy-start(bf16[1024,1024]{1,0:T(8,128)(2,1)} %all-gather.17.cloned.1.call-done) | copy-start | bytes 6291460
  506.5 11.9 %copy-start.9 = (bf16[1,256,1024]{2,1,0:T(8,128)(2,1)S(1)}, bf16[1,256,1024]{2,1,0:T(8,128)(2,1)}, u32[]{:S(2)}) copy-start(bf16[1,256,1024]{2,1,0:T(8,128)(2,1)} %param.21) | copy-start | bytes 1572868
  516.5 8.2 collective-permute-start
  915.7 5.5 copy-start.1
Sparse Core Ops, SparseCore 0:
  12.4 43.7 all-gather.6
  70.3 41.3 reduce-scatter.5
  290.8 69.1 reduce-scatter.7
  439.0 53.9 reduce-scatter.9
Sparse Core Ops, SparseCore 1:
  73.4 59.3 all-gather.10
  135.3 52.1 all-gather.14
  190.1 52.1 all-gather.16
  244.7 40.1 all-gather.8
  286.7 70.4 all-gather.12
  495.1 139.5 all-reduce.5
  640.0 275.7 all-reduce.3
where the time goes:
time: 929 us; the launch traced here: 928 us
  waiting for transfers between devices  738 us (79%)
  matrix products  112 us (12%)
  local copies, waits for them, and re-layouts  49.6 us (5%)
  between operations  15.6 us (2%)
  other arithmetic  10.7 us (1%)
    psum x1, waiting for transfers between devices, local(): out_grad = lax.psum(mix_term, ('section', 'ray', 'dp'))  273 us
    psum x1, waiting for transfers between devices, spread_2(): return lax.psum(jnp.where(mine, value, jnp.zeros_like(value)), axis)  110 us
    all_gather x1, waiting for transfers between devices, local(): lax.all_gather(jnp.dot(latent, flat_pairs, preferred_element_type=jnp.flo...  66.2 us
    unnamed x12, waiting for transfers between devices  53.9 us
    all_gather x1, waiting for transfers between devices, local(): lax.all_gather(dec_out, 'section', axis=0, tiled=True)  51.5 us
    all_gather x1, waiting for transfers between devices, local(): lax.all_gather(normed, 'ray', axis=0, tiled=True)  42.5 us
    reduce_scatter x1, waiting for transfers between devices, local(): lax.psum_scatter(jnp.dot(mixed, w_attn_out, preferred_element_type=jnp.fl...  39.7 us
    all_gather x1, waiting for transfers between devices, local(): lax.all_gather(layer_norm(hidden, gain_two).astype(jnp.bfloat16), 'ray',...  39.2 us
  transfers between devices with their start and end apart: 12, of which 11 were waited for; matrix products, arithmetic and copies ran while one was open for 16% of the time, Pallas kernels for 0%

commit v1 on v0

--- a/solution.py
+++ b/solution.py
@@ -5,6 +5,18 @@
 from jax.sharding import PartitionSpec as P
 
 HEADS = 16
+
+
+def ring_gather(array, axis, dim):
+    ways, here, step = (lax.axis_size(axis), lax.axis_index(axis), array.shape[dim])
+    dims = [n * ways if d == dim else n for d, n in enumerate(array.shape)]
+    full = lax.dynamic_update_slice_in_dim(
+        jnp.zeros(dims, array.dtype), array, here * step, axis=dim
+    )
+    for far in range(1, ways):
+        array = lax.ppermute(array, axis, [(d, (d + 1) % ways) for d in range(ways)])
+        full = lax.dynamic_update_slice_in_dim(full, array, (here - far) % ways * step, axis=dim)
+    return full
 
 
 def shifted(value, axis, by):
@@ -128,11 +140,10 @@
     queries = ray_queries[0]
     cotangent = feature_grad[0]
     flat_pairs = w_pairs.reshape(width, 2 * width)
-    key_values = lax.all_gather(
+    key_values = ring_gather(
         jnp.dot(latent, flat_pairs, preferred_element_type=jnp.float32).astype(jnp.bfloat16),
         "ray",
-        axis=0,
-        tiled=True,
+        0,
     )
     scene_len = key_values.shape[0]
     ray_rows = queries.shape[0]

time: 929 us -> 912 us (0.982)
  waiting for transfers between devices: 738 us -> 706 us
  local copies, waits for them, and re-layouts: 49.6 us -> 60.8 us
    all_gather x1 -> x0, waiting for transfers between devices: 66.2 us -> none  [local(): lax.all_gather(jnp.dot(latent, flat_pairs, preferred_element_type=jnp.flo...]
    ppermute x0 -> x7, waiting for transfers between devices: none -> 60.3 us  [ring_gather(): lax.ppermute(array, axis, [(d, (d + 1) % ways) for d in range(ways)])]
    all_gather x1, waiting for transfers between devices: 39.2 us -> 0.9 us  [local(): lax.all_gather(layer_norm(hidden, gain_two).astype(jnp.bfloat16), 'ray',...]
    all_gather x1, waiting for transfers between devices: 18.6 us -> 47.3 us  [local(): lax.all_gather(dec_kv, 'section', axis=0, tiled=True)]
    all_gather x1, waiting for transfers between devices: 51.5 us -> 27.2 us  [local(): lax.all_gather(dec_out, 'section', axis=0, tiled=True)]
    all_gather x1, waiting for transfers between devices: 39 us -> 49.7 us  [local(): lax.all_gather(dec_query, 'section', axis=0, tiled=True)]
    unnamed x12 -> x11, waiting for transfers between devices: 53.9 us -> 55.6 us
  transfers between devices with their start and end apart: 12 -> 18, of which waited for: 11 -> 15; matrix products, arithmetic and copies ran while one was open for 16% -> 19% of each run, Pallas kernels for 0% -> 0%
where the time goes in v1:
time: 912 us; the launch traced here: 911 us
  waiting for transfers between devices  706 us (77%)
  matrix products  112 us (12%)
  local copies, waits for them, and re-layouts  60.8 us (7%)
  between operations  14.5 us (2%)
  other arithmetic  10.7 us (1%)
    psum x1, waiting for transfers between devices, local(): out_grad = lax.psum(mix_term, ('section', 'ray', 'dp'))  273 us
    psum x1, waiting for transfers between devices, spread_2(): return lax.psum(jnp.where(mine, value, jnp.zeros_like(value)), axis)  111 us
    ppermute x7, waiting for transfers between devices, ring_gather(): lax.ppermute(array, axis, [(d, (d + 1) % ways) for d in range(ways)])  60.3 us
    unnamed x11, waiting for transfers between devices  55.6 us
    all_gather x1, waiting for transfers between devices, local(): lax.all_gather(dec_query, 'section', axis=0, tiled=True)  49.7 us
    all_gather x1, waiting for transfers between devices, local(): lax.all_gather(dec_kv, 'section', axis=0, tiled=True)  47.3 us
    all_gather x1, waiting for transfers between devices, local(): lax.all_gather(normed, 'ray', axis=0, tiled=True)  41.7 us
    dot_general x1, matrix products, local(): jnp.einsum('hrl,rhd->lhd', score_grad, query, preferred_element_type=jnp....  38.2 us
  transfers between devices with their start and end apart: 18, of which 15 were waited for; matrix products, arithmetic and copies ran while one was open for 19% of the time, Pallas kernels for 0%

profile of v1, /device:TPU:2, one launch (start us, length us, event | category | flops | bytes accessed | tf_op | source)
XLA Modules:
  0.0 911.2 jit_solution(8915413487746725635)
XLA Ops:
  7.2 1.1 convert_reduce_fusion.1
  8.4 1.2 fusion.73
  9.6 1.9 fusion.75
  12.3 1.4 copy.61
  13.7 41.7 %all-gather.6.cloned.1.call-done = bf16[1024,1024]{1,0:T(8,128)(2,1)} async-done(((bf16[128,1024]{1,0:T(8,128)(2,1)}), bf16[1024,1024]{1,0:T(8,128)(2,1)}) %all-gather.6.cloned.1.call-update) | async-done | bytes 2097168 | tf_op jit(solution)/shard_map/all_gather | solution.py:101
  55.4 2.6 convolution_convert_fusion.3
  58.0 4.9 fusion.97
  62.9 4.3 fusion.48
  67.2 2.1 convolution_convert_fusion.2
  70.5 47.3 %all-gather.10.cloned.1.call-done = bf16[1024,2,1024]{2,1,0:T(2,128)(2,1)} async-done(((bf16[64,2,1024]{2,1,0:T(2,128)(2,1)}), bf16[1024,2,1024]{2,1,0:T(2,128)(2,1)}) %all-gather.10.cloned.1.call-update) | async-done | bytes 4194320 | tf_op jit(solution)/shard_map/all_gather | solution.py:136
  117.8 11.1 %copy.64 = bf16[1024,2,1024]{0,2,1:T(8,128)(2,1)} copy(bf16[1024,2,1024]{2,1,0:T(2,128)(2,1)} %all-gather.10.cloned.1.call-done) | data formatting | bytes 8388608 | tf_op jit(solution)/shard_map/all_gather | solution.py:136
  129.0 3.9 convolution_convert_fusion
  132.9 1.6 collective-permute-start.1
  134.5 34.4 %reduce-scatter.6.cloned.1.call-done = bf16[128,1024]{1,0:T(8,128)(2,1)} async-done(((bf16[1024,1024]{1,0:T(8,128)(2,1)}), bf16[128,1024]{1,0:T(8,128)(2,1)}) %reduce-scatter.6.cloned.1.call-update) | async-done | bytes 262160 | tf_op jit(solution)/shard_map/reduce_scatter | solution.py:104
  169.0 1.1 convert_reduce_fusion
  170.3 0.9 fusion.72
  171.9 12.2 %collective-permute-done.2 = bf16[128,2048]{1,0:T(8,128)(2,1)} collective-permute-done((bf16[128,2048]{1,0:T(8,128)(2,1)}, bf16[128,2048]{1,0:T(8,128)(2,1)}, u32[]{:S(2)}, u32[]{:S(2)}) %collective-permute-start.2) | collective-permute-done | bytes 524320 | tf_op jit(solution)/shard_map/ppermute | solution.py:17
  184.1 12.1 %collective-permute-done.3 = bf16[128,2048]{1,0:T(8,128)(2,1)} collective-permute-done((bf16[128,2048]{1,0:T(8,128)(2,1)}, bf16[128,2048]{1,0:T(8,128)(2,1)}, u32[]{:S(2)}, u32[]{:S(2)}) %collective-permute-start.3) | collective-permute-done | bytes 524320 | tf_op jit(solution)/shard_map/ppermute | solution.py:17
  196.2 27.2 %all-gather.14.cloned.1.call-done = bf16[1024,1024]{1,0:T(8,128)(2,1)} async-done(((bf16[64,1024]{1,0:T(8,128)(2,1)}), bf16[1024,1024]{1,0:T(8,128)(2,1)}) %all-gather.14.cloned.1.call-update) | async-done | bytes 2097168 | tf_op jit(solution)/shard_map/all_gather | solution.py:137
  223.5 3.1 convolution_convert_fusion.4
  226.6 2.0 copy.74
  228.6 49.7 %all-gather.12.cloned.1.call-done = bf16[1024,1024]{1,0:T(8,128)(2,1)} async-done(((bf16[64,1024]{1,0:T(8,128)(2,1)}), bf16[1024,1024]{1,0:T(8,128)(2,1)}) %all-gather.12.cloned.1.call-update) | async-done | bytes 2097168 | tf_op jit(solution)/shard_map/all_gather | solution.py:135
  278.3 2.3 convolution_convert_fusion.5
  280.7 1.0 copy.73
  281.9 1.8 collective-permute-start.5
  283.8 2.5 broadcast_in_dim.30
  286.3 0.8 constant_dynamic-update-slice_fusion.7
  287.1 1.3 copy.66
  288.4 0.8 constant_dynamic-update-slice_fusion.6
  289.3 1.3 copy.67
  290.6 0.8 constant_dynamic-update-slice_fusion.5
  291.4 1.3 copy.68
  292.7 9.2 %collective-permute-done.5 = bf16[128,2048]{1,0:T(8,128)(2,1)S(1)} collective-permute-done((bf16[128,2048]{1,0:T(8,128)(2,1)}, bf16[128,2048]{1,0:T(8,128)(2,1)S(1)}, u32[]{:S(2)}, u32[]{:S(2)}) %collective-permute-start.5) | collective-permute-done | bytes 524320 | tf_op jit(solution)/shard_map/ppermute | solution.py:17
  303.5 1.3 copy.69
  304.8 0.8 constant_dynamic-update-slice_fusion.3
  305.9 0.8 constant_dynamic-update-slice_fusion.2
  306.7 21.6 %collective-permute-done.6 = bf16[128,2048]{1,0:T(8,128)(2,1)S(1)} collective-permute-done((bf16[128,2048]{1,0:T(8,128)(2,1)S(1)}, bf16[128,2048]{1,0:T(8,128)(2,1)S(1)}, u32[]{:S(2)}, u32[]{:S(2)}) %collective-permute-start.6) | collective-permute-done | bytes 524320 | tf_op jit(solution)/shard_map/ppermute | solution.py:17
  328.6 0.8 constant_dynamic-update-slice_fusion.1
  329.5 0.9 all-gather.8.cloned.1.call-done
  330.4 5.8 convolution_convert_fusion.1
  336.3 5.3 collective-permute-done.7
  341.8 0.8 constant_dynamic-update-slice_fusion
  342.7 4.1 fusion.96
  346.8 8.1 fusion.99
  354.9 9.8 %fusion.98 = (f32[16,256]{1,0:T(8,128)S(1)}, f32[16,256,1024]{2,1,0:T(8,128)}) fusion(bf16[256,16,64]{0,2,1:T(8,128)(2,1)S(1)} %bitcast.149, bf16[1024,16,64]{0,2,1:T(8,128)(2,1)} %bitcast.145), kind=kOutput, calls=%fused_computation.118 | convolution fusion | flops 549454848 | bytes 19415040 | tf_op jit(solution)/shard_map/sub | solution.py:42
  364.7 38.2 %fusion.38 = bf16[16,64,1024]{2,1,0:T(8,128)(2,1)} fusion(bf16[256,16,64]{0,2,1:T(8,128)(2,1)S(1)} %bitcast.150, f32[16,256,1024]{2,1,0:T(8,128)} %fusion.99, f32[16,256,1024]{2,1,0:T(8,128)} %get-tuple-element.18, f32[16,256]{1,0:T(8,128)S(1)} %get-tuple-element.17), kind=kOutput, calls=%fused_computation.40 | convolution fusion | flops 567284736 | bytes 36192256 | tf_op jit(solution)/shard_map/hrl,rhd->lhd/dot_general | solution.py:181
  402.9 7.1 fusion.35
  410.1 2.4 pad_maximum_fusion
  412.4 6.5 copy.80
  419.1 1.9 broadcast_select_fusion
  420.9 53.8 %reduce-scatter.10.cloned.1.call-done = bf16[128,2048]{1,0:T(8,128)(2,1)} async-done(((bf16[1024,2048]{1,0:T(8,128)(2,1)}), bf16[128,2048]{1,0:T(8,128)(2,1)}) %reduce-scatter.10.cloned.1.call-update) | async-done | bytes 524304
  474.7 2.0 copy.81
  477.0 8.5 fusion.42
  485.5 2.7 fusion.78
  488.3 10.0 %fusion.95 = (bf16[1024,1,1024]{2,1,0:T(2,128)(2,1)}, bf16[1024,1,1024]{2,1,0:T(2,128)(2,1)}) fusion(bf16[1024,2,1024]{2,1,0:T(2,128)(2,1)} %all-gather.10.cloned.1.call-done), kind=kLoop, calls=%fused_computation.115 | loop fusion | bytes 8388608 | tf_op jit(solution)/shard_map/slice | solution.py:61
  498.3 1.9 collective-permute-start
  500.2 1.5 fusion.45
  501.8 4.5 collective-permute-done
  506.2 111.3 %all-reduce.6.cloned.1.call-done = (bf16[128,1024]{1,0:T(8,128)(2,1)}, bf16[128,2,1024]{0,2,1:T(8,128)(2,1)}) async-done(((bf16[128,1024]{1,0:T(8,128)(2,1)}, bf16[128,2,1024]{0,2,1:T(8,128)(2,1)}), (bf16[128,1024]{1,0:T(8,128)(2,1)}, bf16[128,2,1024]{0,2,1:T(8,128)(2,1)})) %all-reduce.6.cloned.1.call-update) | async-done | bytes 786448 | tf_op jit(solution)/shard_map/psum | solution.py:30
  617.5 0.8 constant_dynamic-slice_fusion
  619.0 3.1 fusion.33
  622.2 3.9 fusion.49
  626.0 272.9 %all-reduce.4.cloned.1.call-done = f32[1024,1024]{1,0:T(8,128)} async-done(((f32[1024,1024]{1,0:T(8,128)}), f32[1024,1024]{1,0:T(8,128)}) %all-reduce.4.cloned.1.call-update) | async-done | bytes 4194320 | tf_op jit(solution)/shard_map/psum | solution.py:172
  899.6 4.8 copy.107
  (70 shorter events, 7.5 us)
Async XLA Ops:
  7.2 323.2 %copy-start = (bf16[1,512,1024]{2,1,0:T(8,128)(2,1)S(1)}, bf16[1,512,1024]{2,1,0:T(8,128)(2,1)}, u32[]{:S(2)}) copy-start(bf16[1,512,1024]{2,1,0:T(8,128)(2,1)} %param.19) | copy-start | bytes 3145732
  7.2 48.2 %all-gather.6.cloned.1.call-start = ((), (), s32[]{:S(2)}) async-start(), calls=%async_computation.3 | async-start | bytes 2359296 | tf_op jit(solution)/shard_map/all_gather | solution.py:101
  11.5 106.4 %all-gather.10.cloned.1.call-start = ((), (), s32[]{:S(2)}) async-start(), calls=%async_computation.7 | async-start | bytes 4456448 | tf_op jit(solution)/shard_map/all_gather | solution.py:136
  12.2 156.7 %reduce-scatter.6.cloned.1.call-start = ((), (), s32[]{:S(2)}) async-start(), calls=%async_computation.4 | async-start | bytes 2359296 | tf_op jit(solution)/shard_map/reduce_scatter | solution.py:104
  62.9 4.3 copy-start.11
  69.3 154.1 %all-gather.14.cloned.1.call-start = ((), (), s32[]{:S(2)}) async-start(), calls=%async_computation.9 | async-start | bytes 2228224 | tf_op jit(solution)/shard_map/all_gather | solution.py:137
  69.9 208.4 %all-gather.12.cloned.1.call-start = ((), (), s32[]{:S(2)}) async-start(), calls=%async_computation.8 | async-start | bytes 2228224 | tf_op jit(solution)/shard_map/all_gather | solution.py:135
  70.5 58.5 %copy-start.12 = (bf16[1,128,1024]{2,1,0:T(8,128)(2,1)S(1)}, bf16[1,128,1024]{2,1,0:T(8,128)(2,1)}, u32[]{:S(2)}) copy-start(bf16[1,128,1024]{2,1,0:T(8,128)(2,1)} %param.20) | copy-start | bytes 786436
  70.5 259.9 %all-gather.8.cloned.1.call-start = ((), (), s32[]{:S(2)}) async-start(), calls=%async_computation.5 | async-start | bytes 2359296 | tf_op jit(solution)/shard_map/all_gather | solution.py:113
  129.0 40.0 %copy-start.2 = (bf16[1,1,128,1024]{3,2,1,0:T(8,128)(2,1)S(1)}, bf16[1,1,128,1024]{3,2,1,0:T(8,128)(2,1)}, u32[]{:S(2)}) copy-start(bf16[1,1,128,1024]{3,2,1,0:T(8,128)(2,1)} %param.13) | copy-start | bytes 786436
  129.0 41.4 %copy-start.14 = (f32[1,1024]{1,0:T(1,128)S(1)}, f32[1,1024]{1,0:T(1,128)}, u32[]{:S(2)}) copy-start(f32[1,1024]{1,0:T(1,128)} %param.17) | copy-start | bytes 12292
  129.0 94.5 %copy-start.6 = (bf16[1,256,1024]{2,1,0:T(8,128)(2,1)S(1)}, bf16[1,256,1024]{2,1,0:T(8,128)(2,1)}, u32[]{:S(2)}) copy-start(bf16[1,256,1024]{2,1,0:T(8,128)(2,1)} %param.25) | copy-start | bytes 1572868
  132.9 145.5 %copy-start.8 = (bf16[1,256,1024]{2,1,0:T(8,128)(2,1)S(1)}, bf16[1,256,1024]{2,1,0:T(8,128)(2,1)}, u32[]{:S(2)}) copy-start(bf16[1,256,1024]{2,1,0:T(8,128)(2,1)} %param.21) | copy-start | bytes 1572868
  132.9 38.4 %collective-permute-start.1 = (bf16[128,2048]{1,0:T(8,128)(2,1)S(1)}, bf16[128,2048]{1,0:T(8,128)(2,1)}, u32[]{:S(2)}, u32[]{:S(2)}) collective-permute-start(bf16[128,2048]{1,0:T(8,128)(2,1)S(1)} %convolution_convert_fusion), channel_id=1, source_target_pairs={{0,2},{2,4},{4,6},{6,8},{8,10},{10,12},{12,14},{14,0},{1,3},{3,5},... | collective-permute-start | bytes 1572872 | tf_op jit(solution)/shard_map/ppermute | solution.py:17
  171.3 247.8 %reduce-scatter.8.cloned.1.call-start = ((), (), s32[]{:S(2)}) async-start(), calls=%async_computation.6 | async-start | bytes 2359296 | tf_op jit(solution)/shard_map/reduce_scatter | solution.py:121
  171.3 12.8 %collective-permute-start.2 = (bf16[128,2048]{1,0:T(8,128)(2,1)}, bf16[128,2048]{1,0:T(8,128)(2,1)}, u32[]{:S(2)}, u32[]{:S(2)}) collective-permute-start(bf16[128,2048]{1,0:T(8,128)(2,1)} %collective-permute-done.1), channel_id=1, source_target_pairs={{0,2},{2,4},{4,6},{6,8},{8,10},{10,12},{12,14},{14,0},{1,3},{3,5},... | collective-permute-start | bytes 1572872 | tf_op jit(solution)/shard_map/ppermute | solution.py:17
  184.1 12.1 %collective-permute-start.3 = (bf16[128,2048]{1,0:T(8,128)(2,1)}, bf16[128,2048]{1,0:T(8,128)(2,1)}, u32[]{:S(2)}, u32[]{:S(2)}) collective-permute-start(bf16[128,2048]{1,0:T(8,128)(2,1)} %collective-permute-done.2), channel_id=1, source_target_pairs={{0,2},{2,4},{4,6},{6,8},{8,10},{10,12},{12,14},{14,0},{1,3},{3,5},... | collective-permute-start | bytes 1572872 | tf_op jit(solution)/shard_map/ppermute | solution.py:17
  196.2 85.7 %collective-permute-start.4 = (bf16[128,2048]{1,0:T(8,128)(2,1)}, bf16[128,2048]{1,0:T(8,128)(2,1)}, u32[]{:S(2)}, u32[]{:S(2)}) collective-permute-start(bf16[128,2048]{1,0:T(8,128)(2,1)} %collective-permute-done.3), channel_id=1, source_target_pairs={{0,2},{2,4},{4,6},{6,8},{8,10},{10,12},{12,14},{14,0},{1,3},{3,5},... | collective-permute-start | bytes 1572872 | tf_op jit(solution)/shard_map/ppermute | solution.py:17
  281.9 20.0 %collective-permute-start.5 = (bf16[128,2048]{1,0:T(8,128)(2,1)}, bf16[128,2048]{1,0:T(8,128)(2,1)S(1)}, u32[]{:S(2)}, u32[]{:S(2)}) collective-permute-start(bf16[128,2048]{1,0:T(8,128)(2,1)} %collective-permute-done.4), channel_id=1, source_target_pairs={{0,2},{2,4},{4,6},{6,8},{8,10},{10,12},{12,14},{14,0},{1,3},{3,5},... | collective-permute-start | bytes 1572872 | tf_op jit(solution)/shard_map/ppermute | solution.py:17
  301.9 26.4 %collective-permute-start.6 = (bf16[128,2048]{1,0:T(8,128)(2,1)S(1)}, bf16[128,2048]{1,0:T(8,128)(2,1)S(1)}, u32[]{:S(2)}, u32[]{:S(2)}) collective-permute-start(bf16[128,2048]{1,0:T(8,128)(2,1)S(1)} %collective-permute-done.5), channel_id=1, source_target_pairs={{0,2},{2,4},{4,6},{6,8},{8,10},{10,12},{12,14},{14,0},{1,3},{3,5},... | collective-permute-start | bytes 1572872 | tf_op jit(solution)/shard_map/ppermute | solution.py:17
  328.6 13.0 %collective-permute-start.7 = (bf16[128,2048]{1,0:T(8,128)(2,1)S(1)}, bf16[128,2048]{1,0:T(8,128)(2,1)S(1)}, u32[]{:S(2)}, u32[]{:S(2)}) collective-permute-start(bf16[128,2048]{1,0:T(8,128)(2,1)S(1)} %collective-permute-done.6), channel_id=1, source_target_pairs={{0,2},{2,4},{4,6},{6,8},{8,10},{10,12},{12,14},{14,0},{1,3},{3,5},... | collective-permute-start | bytes 1572872 | tf_op jit(solution)/shard_map/ppermute | solution.py:17
  336.2 138.4 %reduce-scatter.10.cloned.1.call-start = ((), (), s32[]{:S(2)}) async-start(), calls=%async_computation.11 | async-start | bytes 4718592
  342.7 4.1 copy-start.4
  346.8 8.1 copy-start.10
  402.9 7.1 copy-start.5
  419.0 198.5 %all-reduce.6.cloned.1.call-start = ((), (), s32[]{:S(2)}) async-start(), calls=%async_computation.12 | async-start | bytes 1572864 | tf_op jit(solution)/shard_map/psum | solution.py:30
  476.7 8.8 copy-start.7
  476.7 422.2 %all-reduce.4.cloned.1.call-start = ((), (), s32[]{:S(2)}) async-start(), calls=%async_computation.10 | async-start | bytes 8388608 | tf_op jit(solution)/shard_map/psum | solution.py:172
  488.2 10.0 %copy-start.13 = (bf16[128,1024]{1,0:T(8,128)(2,1)S(1)}, bf16[128,1024]{1,0:T(8,128)(2,1)}, u32[]{:S(2)}) copy-start(bf16[128,1024]{1,0:T(8,128)(2,1)} %get-tuple-element.8) | copy-start | bytes 786436
  488.3 12.0 %copy-start.3 = (bf16[1024,1024]{1,0:T(8,128)(2,1)S(1)}, bf16[1024,1024]{1,0:T(8,128)(2,1)}, u32[]{:S(2)}) copy-start(bf16[1024,1024]{1,0:T(8,128)(2,1)} %all-gather.14.cloned.1.call-done) | copy-start | bytes 6291460
  488.3 12.0 %copy-start.9 = (bf16[1,256,1024]{2,1,0:T(8,128)(2,1)S(1)}, bf16[1,256,1024]{2,1,0:T(8,128)(2,1)}, u32[]{:S(2)}) copy-start(bf16[1,256,1024]{2,1,0:T(8,128)(2,1)} %param.21) | copy-start | bytes 1572868
  498.3 8.0 collective-permute-start
  898.9 5.5 copy-start.1
Sparse Core Ops, SparseCore 0:
  11.6 43.7 all-gather.5
  58.2 59.6 all-gather.9
  120.4 48.5 reduce-scatter.5
  171.6 51.8 all-gather.13
  226.0 52.2 all-gather.11
  280.6 49.7 all-gather.7
  336.3 41.9 reduce-scatter.7
  419.1 55.5 reduce-scatter.9
  477.9 139.5 all-reduce.5
  622.8 276.0 all-reduce.3
